TPU v7x, 256 devices: a whole 4x4x8 slice. The times are simulated.
256 devices in a mesh: blk: 64 (over y, z, x_hi), bin: 4 (over x_lo, core).
Axes of the slice: x: 4 (x_hi: 2, x_lo: 2; x = x_hi * 2 + x_lo), y: 4, z: 8, core: 2. Of those that a mesh axis runs over, the one named last changes fastest.
Arguments:
- spectrum: float32 [64, 8, 12, 512, 128], P('bin', None, None, 'blk'), may hold values from 0.05 to 2
- wind: float32 [8, 12, 128], replicated, may hold values from -12 to 12
- fall_speed: float32 [64], P('bin'), may hold values from 0.1 to 10
- collection: bfloat16 [64, 64, 64], P(None, None, 'bin'), may hold values from -0.09375 to 0.09375
- act_order: int32 [64, 8], P('blk'), may hold values from 0 to 7, each once within a row
- act_count: int32 [64], P('blk'), may hold values from 1 to 4, as said below
Outputs:
- updated: float32 [64, 8, 12, 512, 128], P('bin', None, None, 'blk')
Inputs may be any that keep to these rules, and one draw needn't show every extreme that they name: `act_order`: each row names every block row once; the active ones are its first act_count entries. `act_count`: some column holds exactly half of 8 active blocks.
All inputs are finite; a program needn't handle non-finite values.
Results may differ from a plain program's by a relative error of at most 0.0055.
Values may be sent and summed in bfloat16 or wider, within the bound.
A program may use at most 128 MiB of HBM per device.

v0:
```python
import jax
import jax.numpy as jnp
from jax import lax
from jax.sharding import PartitionSpec as P

weno_eps = 1e-06
courant = 0.04
time_step = 2.0


def padded_2(cells, sides, width):
    for axis, dim in sides:
        count = lax.axis_size(axis)
        ends = count - 1
        head = lax.slice_in_dim(cells, 0, width, axis=dim)
        tail = lax.slice_in_dim(cells, cells.shape[dim] - width, cells.shape[dim], axis=dim)
        cells = jnp.concatenate(
            [
                lax.ppermute(tail, axis, [(i, (i + 1) % count) for i in range(ends)]),
                cells,
                lax.ppermute(head, axis, [((i + 1) % count, i) for i in range(ends)]),
            ],
            axis=dim,
        )
    return cells


def reconstruct(first, second, third, fourth, fifth):
    cand_left = (2.0 * first - 7.0 * second + 11.0 * third) / 6.0
    cand_mid = (-second + 5.0 * third + 2.0 * fourth) / 6.0
    cand_right = (2.0 * third + 5.0 * fourth - fifth) / 6.0
    smooth_left = (
        13.0 / 12.0 * (first - 2.0 * second + third) ** 2
        + 0.25 * (first - 4.0 * second + 3.0 * third) ** 2
    )
    smooth_mid = 13.0 / 12.0 * (second - 2.0 * third + fourth) ** 2 + 0.25 * (second - fourth) ** 2
    smooth_right = (
        13.0 / 12.0 * (third - 2.0 * fourth + fifth) ** 2
        + 0.25 * (3.0 * third - 4.0 * fourth + fifth) ** 2
    )
    weight_left = 0.1 / (weno_eps + smooth_left) ** 2
    weight_mid = 0.6 / (weno_eps + smooth_mid) ** 2
    weight_right = 0.3 / (weno_eps + smooth_right) ** 2
    total = weight_left + weight_mid + weight_right
    return (weight_left * cand_left + weight_mid * cand_mid + weight_right * cand_right) / total


def face_terms(padded, width, wind):

    def window(offset):
        return lax.slice_in_dim(padded, offset, offset + width + 1, axis=3)

    upwind_pos = reconstruct(window(0), window(1), window(2), window(3), window(4))
    upwind_neg = reconstruct(window(5), window(4), window(3), window(2), window(1))
    speed = wind[None, :, :, None, :]
    return (speed, speed * upwind_pos, speed * upwind_neg)


def sediment(field, fall_speed):
    above = jnp.concatenate([field[:, :, 1:], jnp.zeros_like(field[:, :, :1])], axis=2)
    return field - courant * fall_speed[:, None, None, None, None] * (field - above)


def collide(spectra, table):
    count_in = spectra.shape[0]
    planes = spectra.shape[1] * spectra.shape[2]
    flat = spectra.reshape(count_in, planes, -1)
    out_bins = table.shape[1] // count_in

    def one_plane(index):
        cells = lax.dynamic_index_in_dim(flat, index, 1, keepdims=False)
        inner = lax.dot_general(
            table, cells, (((0,), (0,)), ((), ())), preferred_element_type=jnp.float32
        )
        inner = inner.astype(jnp.bfloat16).reshape(count_in, out_bins, -1)
        return jnp.einsum("ic,ikc->kc", cells, inner, preferred_element_type=jnp.float32)

    result = lax.map(one_plane, jnp.arange(planes, dtype=jnp.int32))
    return jnp.moveaxis(result, 0, 1).reshape((out_bins,) + spectra.shape[1:])


def local(spectrum, wind, fall_speed, collection, act_order, act_count):
    width = spectrum.shape[3]
    padded = padded_2(spectrum, (("blk", 3),), 3)
    speed, flux_pos, flux_neg = face_terms(padded, width, wind)
    flux = jnp.where(speed > 0, flux_pos, flux_neg)
    advected = spectrum - courant * (flux[:, :, :, 1:, :] - flux[:, :, :, :-1, :])
    settled = sediment(advected, fall_speed)
    slots = spectrum.shape[1]
    capacity = slots // 2
    order = act_order[0, :capacity]
    picked = jnp.take(settled, order, axis=1).astype(jnp.bfloat16)
    all_bins = collection.shape[0]
    whole = lax.all_gather(picked, "bin", axis=0, tiled=True)
    tendency = collide(whole, collection.reshape(all_bins, -1))
    entries = jnp.arange(capacity, dtype=jnp.int32)
    slot_ids = jnp.arange(slots, dtype=jnp.int32)
    chosen = jnp.logical_and(order[:, None] == slot_ids[None, :], (entries < act_count[0])[:, None])
    update = jnp.einsum("as,bazxy->bszxy", chosen.astype(jnp.float32), tendency)
    return settled + time_step * update


def solution(mesh):
    return jax.shard_map(
        local,
        mesh=mesh,
        in_specs=(
            P("bin", None, None, "blk", None),
            P(),
            P("bin"),
            P(None, None, "bin"),
            P("blk", None),
            P("blk"),
        ),
        out_specs=P("bin", None, None, "blk", None),
        check_vma=False,
    )
```

profile of v0, /device:TPU:1, one launch (start us, length us, event | category | flops | bytes accessed | tf_op | source)
XLA Modules:
  0.0 556.1 jit_solution(7151124852510900609)
XLA Ops:
  6.5 6.3 %fusion.39 = (f32[16,8,12,3,128]{4,3,2,1,0:T(4,128)S(1)}, f32[16,8,12,3,128]{4,3,2,1,0:T(4,128)S(1)}) fusion(f32[16,8,12,8,128]{4,3,2,1,0:T(8,128)} %param.8), kind=kLoop, calls=%fused_computation.63 | loop fusion | bytes 9437184 | tf_op jit(solution)/shard_map/slice | solution.py:16
  13.6 5.6 %collective-permute-start = (f32[16,8,12,3,128]{4,1,3,2,0:T(8,128)S(1)}, f32[16,8,12,3,128]{4,1,3,2,0:T(8,128)S(1)}, u32[]{:S(2)}, u32[]{:S(2)}) collective-permute-start(f32[16,8,12,3,128]{4,1,3,2,0:T(8,128)S(1)} %copy.47), channel_id=1, source_target_pairs={{0,4},{4,8},{8,12},{12,16},{16,20},{20,24},{24,28},{28,32},{32,36}... | collective-permute-start | bytes 7077896 | tf_op jit(solution)/shard_map/ppermute | solution.py:19
  19.2 2.2 copy.46
  22.8 96.8 %collective-permute-done = f32[16,8,12,3,128]{4,1,3,2,0:T(8,128)S(1)} collective-permute-done((f32[16,8,12,3,128]{4,1,3,2,0:T(8,128)S(1)}, f32[16,8,12,3,128]{4,1,3,2,0:T(8,128)S(1)}, u32[]{:S(2)}, u32[]{:S(2)}) %collective-permute-start) | collective-permute-done | bytes 2359328 | tf_op jit(solution)/shard_map/ppermute | solution.py:19
  119.7 7.7 %constant_dynamic-update-slice_fusion = (f32[16,8,12,11,128]{4,1,3,2,0:T(8,128)S(1)}, f32[16,8,12,11,128]{4,1,3,2,0:T(8,128)S(1)}) fusion(f32[16,8,12,11,128]{4,1,3,2,0:T(8,128)S(1)} %constant_dynamic-update-slice_fusion.1, f32[16,8,12,8,128]{4,3,2,1,0:T(8,128)} %param.8), kind=kLoop, calls=%fused_computation.46 | loop fusion | bytes 18874368 | tf_op jit(solution)/shard_map/concatenate | solution.py:17
  127.4 2.0 constant_dynamic-update-slice_fusion.2
  129.5 32.5 %multiply_select_fusion = f32[16,8,12,9,128]{4,1,3,2,0:T(8,128)} fusion(f32[16,8,12,11,128]{4,1,3,2,0:T(8,128)S(1)} %constant_dynamic-update-slice_fusion.2, f32[16,8,12,11,128]{4,1,3,2,0:T(8,128)S(1)} %get-tuple-element.48, f32[8,12,128]{2,0,1:T(8,128)S(1)} %copy-done.2, pred[8,12,128]{2,0,1:T(8,128)(4,1)S(1)} %broadcast_compare_fusion), kind=kLoop, calls=%fused_computation.8 | loop fusion | flops 224722944 | bytes 49606656 | tf_op jit(solution)/shard_map/jit(_where)/select_n | solution.py:86
  161.9 8.9 %fusion.27 = f32[16,8,12,8,128]{4,1,3,2,0:T(8,128)S(1)} fusion(f32[16,8,12,9,128]{4,1,3,2,0:T(8,128)} %multiply_select_fusion, f32[16,8,12,8,128]{4,3,2,1,0:T(8,128)S(1)} %bitcast.62), kind=kLoop, calls=%fused_computation.38 | loop fusion | flops 4718592 | bytes 25165824 | tf_op jit(solution)/shard_map/sub | solution.py:87
  171.8 2.4 multiply_subtract_fusion.2
  174.2 2.7 copy-done
  178.1 1.9 gather_fusion
  180.0 2.9 fusion.32
  184.2 70.7 %all-gather.2.cloned.1.call-done = bf16[64,4,12,8,128]{4,3,2,0,1:T(8,128)(2,1)} async-done(((bf16[16,4,12,8,128]{4,3,2,0,1:T(8,128)(2,1)}), bf16[64,4,12,8,128]{4,3,2,0,1:T(8,128)(2,1)}) %all-gather.2.cloned.1.call-update) | async-done | bytes 6291472 | tf_op jit(solution)/shard_map/all_gather | solution.py:94
  254.9 7.1 %copy.34 = bf16[64,4,12,8,128]{4,3,0,2,1:T(8,128)(2,1)} copy(bf16[64,4,12,8,128]{4,3,2,0,1:T(8,128)(2,1)} %all-gather.2.cloned.1.call-done) | data formatting | bytes 12582912 | tf_op jit(solution)/shard_map/while | solution.py:78
  262.0 10.3 %reshape.70 = bf16[64,48,1024]{2,0,1:T(8,128)(2,1)} reshape(bf16[64,4,12,8,128]{4,3,0,2,1:T(8,128)(2,1)} %copy.34) | data formatting | bytes 12582912 | tf_op jit(solution)/shard_map/while | solution.py:78
  272.3 268.3 %while.10 = (s32[]{:T(128)}, bf16[48,16,1024]{2,1,0:T(8,128)(2,1)S(1)}, s32[48]{0:T(128)S(1)}, bf16[64,48,1024]{2,0,1:T(8,128)(2,1)}, bf16[64,1024]{1,0:T(8,128)(2,1)S(1)}, /*index=5*/s32[]{:T(128)}, s32[]{:T(128)}, s32[]{:T(128)}) while((s32[]{:T(128)}, bf16[48,16,1024]{2,1,0:T(8,128)(2,1)S(1)}, s32[48]{0:T(128)S(1)}, ...), condition=%wide.region_1.2_spmd, body=%wide.region_0.1_spmd.sunk | while | flops 138461184 | bytes 5210255 | solution.py:78
  274.6 1.7 convolution_convert_fusion.2
  285.7 1.7 convolution_convert_fusion.2
  291.3 1.7 convolution_convert_fusion.2
  296.9 1.7 convolution_convert_fusion.2
  302.5 1.7 convolution_convert_fusion.2
  308.1 1.7 convolution_convert_fusion.2
  313.7 1.7 convolution_convert_fusion.2
  319.3 1.7 convolution_convert_fusion.2
  330.4 1.7 convolution_convert_fusion.2
  336.0 1.7 convolution_convert_fusion.2
  352.8 1.7 convolution_convert_fusion.2
  358.4 1.7 convolution_convert_fusion.2
  363.9 1.7 convolution_convert_fusion.2
  375.1 1.7 convolution_convert_fusion.2
  380.7 1.7 convolution_convert_fusion.2
  397.5 1.7 convolution_convert_fusion.2
  403.0 1.7 convolution_convert_fusion.2
  419.8 1.7 convolution_convert_fusion.2
  425.4 1.7 convolution_convert_fusion.2
  442.1 1.7 convolution_convert_fusion.2
  447.7 1.7 convolution_convert_fusion.2
  464.5 1.7 convolution_convert_fusion.2
  470.1 1.7 convolution_convert_fusion.2
  481.2 1.7 convolution_convert_fusion.2
  486.8 1.7 convolution_convert_fusion.2
  492.4 1.7 convolution_convert_fusion.2
  509.2 1.7 convolution_convert_fusion.2
  514.7 1.7 convolution_convert_fusion.2
  531.5 1.7 convolution_convert_fusion.2
  537.1 1.7 convolution_convert_fusion.2
  541.1 4.4 bitcast_add_fusion
  545.5 3.8 copy.26
  (244 shorter events, 141.7 us)
Async XLA Ops:
  6.5 248.3 %all-gather.2.cloned.1.call-start = ((), (), s32[]{:S(2)}) async-start(), calls=%async_computation | async-start | bytes 7864320 | tf_op jit(solution)/shard_map/all_gather | solution.py:94
  12.8 9.9 %copy-start.4 = (s32[1,8]{1,0:T(1,128)S(1)}, s32[1,8]{1,0:T(1,128)}, u32[]{:S(2)}) copy-start(s32[1,8]{1,0:T(1,128)} %param.12) | copy-start | bytes 100
  12.8 9.9 %copy-start.3 = (f32[16]{0:T(128)S(1)}, f32[16]{0:T(128)}, u32[]{:S(2)}) copy-start(f32[16]{0:T(128)} %param.10) | copy-start | bytes 196
  12.8 9.9 %copy-start.2 = (f32[8,12,128]{2,0,1:T(8,128)S(1)}, f32[8,12,128]{2,0,1:T(8,128)}, u32[]{:S(2)}) copy-start(f32[8,12,128]{2,0,1:T(8,128)} %param.9) | copy-start | bytes 147460
  13.6 105.9 %collective-permute-start = (f32[16,8,12,3,128]{4,1,3,2,0:T(8,128)S(1)}, f32[16,8,12,3,128]{4,1,3,2,0:T(8,128)S(1)}, u32[]{:S(2)}, u32[]{:S(2)}) collective-permute-start(f32[16,8,12,3,128]{4,1,3,2,0:T(8,128)S(1)} %copy.47), channel_id=1, source_target_pairs={{0,4},{4,8},{8,12},{12,16},{16,20},{20,24},{24,28},{28,32},{32,36}... | collective-permute-start | bytes 7077896 | tf_op jit(solution)/shard_map/ppermute | solution.py:19
  21.4 106.0 %collective-permute-start.1 = (f32[16,8,12,3,128]{4,1,3,2,0:T(8,128)}, f32[16,8,12,3,128]{4,1,3,2,0:T(8,128)}, u32[]{:S(2)}, u32[]{:S(2)}) collective-permute-start(f32[16,8,12,3,128]{4,1,3,2,0:T(8,128)} %copy.46), channel_id=1, source_target_pairs={{4,0},{8,4},{12,8},{16,12},{20,16},{24,20},{28,24},{32,28},{36,32}... | collective-permute-start | bytes 7077896 | tf_op jit(solution)/shard_map/ppermute | solution.py:21
  127.4 34.5 %slice-start = ((s8[6291456]{0:T(1024)(128)(4,1)}), s8[4194304]{0:T(1024)(128)(4,1)S(1)}, s32[]{:S(2)}) async-start(s8[6291456]{0:T(1024)(128)(4,1)} %bitcast.61), calls=%async_computation.1 | async-start | bytes 8388608
  129.4 32.5 %slice-start.1 = ((s8[6291456]{0:T(1024)(128)(4,1)}), s8[2097152]{0:T(1024)(128)(4,1)S(1)}, s32[]{:S(2)}) async-start(s8[6291456]{0:T(1024)(128)(4,1)} %bitcast.61), calls=%async_computation.2 | async-start | bytes 4194304
  174.2 2.7 copy-start
  176.9 6.1 %copy-start.1 = (bf16[64,64,16]{1,2,0:T(8,128)(2,1)S(1)}, bf16[64,64,16]{1,2,0:T(8,128)(2,1)}, u32[]{:S(2)}) copy-start(bf16[64,64,16]{1,2,0:T(8,128)(2,1)} %param.11) | copy-start | bytes 393220
Sparse Core Ops, SparseCore 0:
  183.1 71.7 all-gather.1
where the time goes:
time: 559 us; the launch traced here: 556 us
  waiting for transfers between devices  167 us (30%)
  other arithmetic  125 us (22%)
  matrix products  84 us (15%)
  loops' own time  82.2 us (15%)
  local copies, waits for them, and re-layouts  76.2 us (14%)
  between operations  14.3 us (3%)
  starting transfers between devices  6.91 us (1%)
    ppermute x1, waiting for transfers between devices, padded_2(): lax.ppermute(tail, axis, [(i, (i + 1) % count) for i in range(ends)])  96.8 us
    another operation x1, loops' own time, collide(): result = lax.map(one_plane, jnp.arange(planes, dtype=jnp.int32))  82.2 us
    dot_general x48, matrix products, one_plane(): lax.dot_general(table, cells, (((0,), (0,)), ((), ())), preferred_element...  79.6 us
    all_gather x1, waiting for transfers between devices, local(): whole = lax.all_gather(picked, 'bin', axis=0, tiled=True)  70.7 us
    while x48, other arithmetic  44.6 us
    dot_general x48, other arithmetic, one_plane(): jnp.einsum('ic,ikc->kc', cells, inner, preferred_element_type=jnp.float32)  33.7 us
    select_n x1, other arithmetic, local(): flux = jnp.where(speed > 0, flux_pos, flux_neg)  32.5 us
    dynamic_slice x48, local copies, waits for them, and re-layouts, collide(): result = lax.map(one_plane, jnp.arange(planes, dtype=jnp.int32))  27.8 us
  transfers between devices with their start and end apart: 3, of which 2 were waited for; matrix products, arithmetic and copies ran while one was open for 2% of the time, Pallas kernels for 0%

commit v1 on v0

--- a/solution.py
+++ b/solution.py
@@ -91,7 +91,10 @@
     order = act_order[0, :capacity]
     picked = jnp.take(settled, order, axis=1).astype(jnp.bfloat16)
     all_bins = collection.shape[0]
-    whole = lax.all_gather(picked, "bin", axis=0, tiled=True)
+    work_sites = lambda frame_in: jnp.concatenate(
+        lax.all_to_all(jnp.stack(lax.axis_size("bin") * [frame_in]), "bin", 0, 0), axis=0
+    )
+    whole = work_sites(picked)
     tendency = collide(whole, collection.reshape(all_bins, -1))
     entries = jnp.arange(capacity, dtype=jnp.int32)
     slot_ids = jnp.arange(slots, dtype=jnp.int32)

time: 559 us -> 579 us (1.036)
  loops' own time: 82.2 us -> 101 us
  between operations: 14.3 us -> 0.91 us
  local copies, waits for them, and re-layouts: 76.2 us -> 85.9 us
  starting transfers between devices: 6.91 us -> 13.8 us
    all_gather x1 -> x0, waiting for transfers between devices: 70.7 us -> none  [local(): whole = lax.all_gather(picked, 'bin', axis=0, tiled=True)]
    all_to_all x0 -> x1, waiting for transfers between devices: none -> 68.7 us  [local(): lax.all_to_all(jnp.stack(lax.axis_size('bin') * [frame_in]), 'bin', 0, 0)]
    another operation x1, loops' own time: 82.2 us -> 101 us  [collide(): result = lax.map(one_plane, jnp.arange(planes, dtype=jnp.int32))]
    all_to_all x0 -> x1, starting transfers between devices: none -> 6.88 us  [local(): lax.all_to_all(jnp.stack(lax.axis_size('bin') * [frame_in]), 'bin', 0, 0)]
where the time goes in v1:
time: 579 us; the launch traced here: 575 us
  waiting for transfers between devices  165 us (28%)
  other arithmetic  124 us (21%)
  loops' own time  101 us (17%)
  local copies, waits for them, and re-layouts  85.9 us (15%)
  matrix products  84 us (15%)
  starting transfers between devices  13.8 us (2%)
    another operation x1, loops' own time, collide(): result = lax.map(one_plane, jnp.arange(planes, dtype=jnp.int32))  101 us
    ppermute x1, waiting for transfers between devices, padded_2(): lax.ppermute(tail, axis, [(i, (i + 1) % count) for i in range(ends)])  96.8 us
    dot_general x48, matrix products, one_plane(): lax.dot_general(table, cells, (((0,), (0,)), ((), ())), preferred_element...  79.6 us
    all_to_all x1, waiting for transfers between devices, local(): lax.all_to_all(jnp.stack(lax.axis_size('bin') * [frame_in]), 'bin', 0, 0)  68.7 us
    while x48, other arithmetic  44.6 us
    dot_general x48, other arithmetic, one_plane(): jnp.einsum('ic,ikc->kc', cells, inner, preferred_element_type=jnp.float32)  33.7 us
    select_n x1, other arithmetic, local(): flux = jnp.where(speed > 0, flux_pos, flux_neg)  32.5 us
    dynamic_slice x48, local copies, waits for them, and re-layouts, collide(): result = lax.map(one_plane, jnp.arange(planes, dtype=jnp.int32))  31.9 us
  transfers between devices with their start and end apart: 3, of which 2 were waited for; matrix products, arithmetic and copies ran while one was open for 2% of the time, Pallas kernels for 0%

profile of v1, /device:TPU:1, one launch (start us, length us, event | category | flops | bytes accessed | tf_op | source)
XLA Modules:
  0.0 575.0 jit_solution(1451489985640293401)
XLA Ops:
  0.0 6.3 %fusion.39 = (f32[16,8,12,3,128]{4,3,2,1,0:T(4,128)S(1)}, f32[16,8,12,3,128]{4,3,2,1,0:T(4,128)S(1)}) fusion(f32[16,8,12,8,128]{4,3,2,1,0:T(8,128)} %param.8), kind=kLoop, calls=%fused_computation.63 | loop fusion | bytes 9437184 | tf_op jit(solution)/shard_map/slice | solution.py:16
  7.1 5.6 collective-permute-start
  12.7 2.2 copy.70
  16.2 96.8 %collective-permute-done = f32[16,8,12,3,128]{4,1,3,2,0:T(8,128)S(1)} collective-permute-done((f32[16,8,12,3,128]{4,1,3,2,0:T(8,128)S(1)}, f32[16,8,12,3,128]{4,1,3,2,0:T(8,128)S(1)}, u32[]{:S(2)}, u32[]{:S(2)}) %collective-permute-start) | collective-permute-done | bytes 2359328 | tf_op jit(solution)/shard_map/ppermute | solution.py:19
  113.2 7.7 %constant_dynamic-update-slice_fusion = (f32[16,8,12,11,128]{4,1,3,2,0:T(8,128)S(1)}, f32[16,8,12,11,128]{4,1,3,2,0:T(8,128)S(1)}) fusion(f32[16,8,12,11,128]{4,1,3,2,0:T(8,128)S(1)} %constant_dynamic-update-slice_fusion.1, f32[16,8,12,8,128]{4,3,2,1,0:T(8,128)} %param.8), kind=kLoop, calls=%fused_computation.46 | loop fusion | bytes 18874368 | tf_op jit(solution)/shard_map/concatenate | solution.py:17
  120.9 2.0 constant_dynamic-update-slice_fusion.2
  122.9 32.5 %multiply_select_fusion = f32[16,8,12,9,128]{4,1,3,2,0:T(8,128)} fusion(f32[16,8,12,11,128]{4,1,3,2,0:T(8,128)S(1)} %constant_dynamic-update-slice_fusion.2, f32[16,8,12,11,128]{4,1,3,2,0:T(8,128)S(1)} %get-tuple-element.58, f32[8,12,128]{2,0,1:T(8,128)S(1)} %copy-done.2, pred[8,12,128]{2,0,1:T(8,128)(4,1)S(1)} %broadcast_compare_fusion), kind=kLoop, calls=%fused_computation.8 | loop fusion | flops 224722944 | bytes 49606656 | tf_op jit(solution)/shard_map/jit(_where)/select_n | solution.py:86
  155.4 8.9 %fusion.27 = f32[16,8,12,8,128]{4,1,3,2,0:T(8,128)S(1)} fusion(f32[16,8,12,9,128]{4,1,3,2,0:T(8,128)} %multiply_select_fusion, f32[16,8,12,8,128]{4,3,2,1,0:T(8,128)S(1)} %bitcast.62), kind=kLoop, calls=%fused_computation.38 | loop fusion | flops 4718592 | bytes 25165824 | tf_op jit(solution)/shard_map/sub | solution.py:87
  165.2 2.4 multiply_subtract_fusion.2
  167.6 2.7 copy-done
  171.5 1.9 gather_fusion
  173.5 1.8 fusion.32
  175.7 4.2 stack.2
  179.9 6.9 %all-to-all-start = ((bf16[4,16,4,12,8,128]{5,4,1,3,2,0:T(8,128)(2,1)}), bf16[4,16,4,12,8,128]{5,4,1,3,2,0:T(8,128)(2,1)}, u32[]{:S(2)}, u32[]{:S(2)}) async-start(bf16[4,16,4,12,8,128]{5,4,1,3,2,0:T(8,128)(2,1)} %stack.2), calls=%async_computation | async-start | bytes 12582912 | tf_op jit(solution)/shard_map/all_to_all | solution.py:95
  188.0 68.7 %all-to-all-done = bf16[4,16,4,12,8,128]{5,4,1,3,2,0:T(8,128)(2,1)} async-done(((bf16[4,16,4,12,8,128]{5,4,1,3,2,0:T(8,128)(2,1)}), bf16[4,16,4,12,8,128]{5,4,1,3,2,0:T(8,128)(2,1)}, u32[]{:S(2)}, u32[]{:S(2)}) %all-to-all-start) | async-done | bytes 6291488 | tf_op jit(solution)/shard_map/all_to_all | solution.py:95
  256.7 8.1 %copy.58 = bf16[4,16,4,12,8,128]{5,4,1,0,3,2:T(8,128)(2,1)} copy(bf16[4,16,4,12,8,128]{5,4,1,3,2,0:T(8,128)(2,1)} %all-to-all-done) | data formatting | bytes 12582912 | tf_op jit(solution)/shard_map/while | solution.py:78
  264.7 10.3 %reshape.68 = bf16[64,48,1024]{2,0,1:T(8,128)(2,1)} reshape(bf16[4,16,4,12,8,128]{5,4,1,0,3,2:T(8,128)(2,1)} %copy.58) | data formatting | bytes 12582912 | tf_op jit(solution)/shard_map/while | solution.py:78
  275.0 291.3 %while.10 = (s32[]{:T(128)}, bf16[48,16,1024]{2,1,0:T(8,128)(2,1)S(1)}, s32[48]{0:T(128)S(1)}, bf16[64,48,1024]{2,0,1:T(8,128)(2,1)}, bf16[64,1024]{1,0:T(8,128)(2,1)S(1)}, /*index=5*/s32[]{:T(128)}, s32[]{:T(128)}, s32[]{:T(128)}) while((s32[]{:T(128)}, bf16[48,16,1024]{2,1,0:T(8,128)(2,1)S(1)}, s32[48]{0:T(128)S(1)}, ...), condition=%wide.region_1.2_spmd, body=%wide.region_0.1_spmd.sunk | while | flops 138461184 | bytes 5210255 | solution.py:78
  277.8 1.7 convolution_convert_fusion.2
  283.9 1.7 convolution_convert_fusion.2
  289.9 1.7 convolution_convert_fusion.2
  296.0 1.7 convolution_convert_fusion.2
  302.1 1.7 convolution_convert_fusion.2
  314.2 1.7 convolution_convert_fusion.2
  320.3 1.7 convolution_convert_fusion.2
  332.4 1.7 convolution_convert_fusion.2
  338.5 1.7 convolution_convert_fusion.2
  350.6 1.7 convolution_convert_fusion.2
  356.7 1.7 convolution_convert_fusion.2
  368.8 1.7 convolution_convert_fusion.2
  374.9 1.7 convolution_convert_fusion.2
  393.1 1.7 convolution_convert_fusion.2
  405.2 1.7 convolution_convert_fusion.2
  411.3 1.7 convolution_convert_fusion.2
  429.5 1.7 convolution_convert_fusion.2
  441.6 1.7 convolution_convert_fusion.2
  447.7 1.7 convolution_convert_fusion.2
  465.9 1.7 convolution_convert_fusion.2
  478.1 1.7 convolution_convert_fusion.2
  484.1 1.7 convolution_convert_fusion.2
  502.3 1.7 convolution_convert_fusion.2
  514.5 1.7 convolution_convert_fusion.2
  520.5 1.7 convolution_convert_fusion.2
  538.7 1.7 convolution_convert_fusion.2
  550.9 1.7 convolution_convert_fusion.2
  557.0 1.7 convolution_convert_fusion.2
  566.8 4.4 bitcast_add_fusion
  571.2 3.8 copy.50
  (245 shorter events, 149.6 us)
Async XLA Ops:
  6.3 9.9 %copy-start.4 = (s32[1,8]{1,0:T(1,128)S(1)}, s32[1,8]{1,0:T(1,128)}, u32[]{:S(2)}) copy-start(s32[1,8]{1,0:T(1,128)} %param.12) | copy-start | bytes 100
  6.3 9.9 %copy-start.3 = (f32[16]{0:T(128)S(1)}, f32[16]{0:T(128)}, u32[]{:S(2)}) copy-start(f32[16]{0:T(128)} %param.10) | copy-start | bytes 196
  6.3 9.9 %copy-start.2 = (f32[8,12,128]{2,0,1:T(8,128)S(1)}, f32[8,12,128]{2,0,1:T(8,128)}, u32[]{:S(2)}) copy-start(f32[8,12,128]{2,0,1:T(8,128)} %param.9) | copy-start | bytes 147460
  7.1 105.9 %collective-permute-start = (f32[16,8,12,3,128]{4,1,3,2,0:T(8,128)S(1)}, f32[16,8,12,3,128]{4,1,3,2,0:T(8,128)S(1)}, u32[]{:S(2)}, u32[]{:S(2)}) collective-permute-start(f32[16,8,12,3,128]{4,1,3,2,0:T(8,128)S(1)} %copy.71), channel_id=1, source_target_pairs={{0,4},{4,8},{8,12},{12,16},{16,20},{20,24},{24,28},{28,32},{32,36}... | collective-permute-start | bytes 7077896 | tf_op jit(solution)/shard_map/ppermute | solution.py:19
  14.9 106.0 %collective-permute-start.1 = (f32[16,8,12,3,128]{4,1,3,2,0:T(8,128)}, f32[16,8,12,3,128]{4,1,3,2,0:T(8,128)}, u32[]{:S(2)}, u32[]{:S(2)}) collective-permute-start(f32[16,8,12,3,128]{4,1,3,2,0:T(8,128)} %copy.70), channel_id=1, source_target_pairs={{4,0},{8,4},{12,8},{16,12},{20,16},{24,20},{28,24},{32,28},{36,32}... | collective-permute-start | bytes 7077896 | tf_op jit(solution)/shard_map/ppermute | solution.py:21
  120.9 34.5 %slice-start = ((s8[6291456]{0:T(1024)(128)(4,1)}), s8[4194304]{0:T(1024)(128)(4,1)S(1)}, s32[]{:S(2)}) async-start(s8[6291456]{0:T(1024)(128)(4,1)} %bitcast.61), calls=%async_computation.1 | async-start | bytes 8388608
  122.9 32.5 %slice-start.1 = ((s8[6291456]{0:T(1024)(128)(4,1)}), s8[2097152]{0:T(1024)(128)(4,1)S(1)}, s32[]{:S(2)}) async-start(s8[6291456]{0:T(1024)(128)(4,1)} %bitcast.61), calls=%async_computation.2 | async-start | bytes 4194304
  167.6 2.7 copy-start
  179.9 6.9 %copy-start.1 = (bf16[64,64,16]{1,2,0:T(8,128)(2,1)S(1)}, bf16[64,64,16]{1,2,0:T(8,128)(2,1)}, u32[]{:S(2)}) copy-start(bf16[64,64,16]{1,2,0:T(8,128)(2,1)} %param.11) | copy-start | bytes 393220
  179.9 76.8 %all-to-all-start = ((bf16[4,16,4,12,8,128]{5,4,1,3,2,0:T(8,128)(2,1)}), bf16[4,16,4,12,8,128]{5,4,1,3,2,0:T(8,128)(2,1)}, u32[]{:S(2)}, u32[]{:S(2)}) async-start(bf16[4,16,4,12,8,128]{5,4,1,3,2,0:T(8,128)(2,1)} %stack.2), calls=%async_computation | async-start | bytes 12582912 | tf_op jit(solution)/shard_map/all_to_all | solution.py:95
